TPU v7x, 256 devices: a whole 4x4x8 slice. The times are simulated.
256 devices in a mesh: row: 8 (over z_lo, y), col: 16 (over z_hi, x), leaf: 2 (over core).
Axes of the slice: x: 4, y: 4, z: 8 (z_hi: 4, z_lo: 2; z = z_hi * 2 + z_lo), core: 2. Of those that a mesh axis runs over, the one named last changes fastest.
Arguments:
- front: float32 [16384, 16384], P('row', ('col', 'leaf')), may hold values from -6 to 6
- child: float32 [16384, 16384], P(('row', 'col', 'leaf')), may hold values from -6 to 6
- row_map: int32 [8, 8], P('row'), may hold values from 0 to 7, each once within a row
- col_map: int32 [64], replicated, may hold values from 0 to 63, each once
- x_fac: float32 [64, 16384], P('row', ('col', 'leaf')), may hold values from -0.75 to 0.75
- w_fac: float32 [64, 16384], P('row', ('col', 'leaf')), may hold values from -0.375 to 0.375
- v_fac: float32 [64, 16384], P(('col', 'leaf'), 'row'), may hold values from -6 to 6
- z_fac: float32 [64, 16384], P(('col', 'leaf'), 'row'), may hold values from -0.75 to 0.75
- dinv: float32 [256, 256], replicated, may hold values from -0.375 to 0.375
- pivots: int32 [256], replicated, may hold values from 0 to 255, each once
- rank_rows: int32 [64], P('row'), may hold values from 16 to 64
- rank_cols: int32 [64], P(('col', 'leaf')), may hold values from 16 to 64
- admissible: int32 [64, 64], P('row', ('col', 'leaf')), may hold values 0 or 1
Outputs:
- updated: float32 [16384, 16384], P('row', ('col', 'leaf'))
Inputs may be any that keep to these rules, and one draw needn't show every extreme that they name: Each row of row_map orders the 8 tile rows of one group; col_map orders all 64 tile columns. `pivots`: A permutation of the panel's columns.
All inputs are finite; a program needn't handle non-finite values. No bound on the sum of `admissible` on one device may be relied on, other than what follows from the above.
Results may differ from a plain program's by a relative error of at most 0.0003.
Values sent between devices are 32-bit elements; how exact they have to be, the bound alone decides.
A program may use at most 128 MiB of HBM per device.

v0:
```python
import jax
import jax.numpy as jnp
from jax import lax
from jax.sharding import PartitionSpec as P

RMAX = 64


def inverse_order(order):
    count = order.shape[0]
    return jnp.zeros((count,), jnp.int32).at[order].set(jnp.arange(count, dtype=jnp.int32))


def on_device(
    front,
    child,
    row_map,
    col_map,
    x_fac,
    w_fac,
    v_fac,
    z_fac,
    dinv,
    pivots,
    rank_rows,
    rank_cols,
    admissible,
):
    highest = lax.Precision.HIGHEST
    tile = dinv.shape[0]
    row_tiles = front.shape[0] // tile
    col_tiles = front.shape[1] // tile
    col_width = front.shape[1]
    all_cols = col_map.shape[0]
    local_rows = child.shape[0]
    col_count = lax.axis_size("col")
    leaf_count = lax.axis_size("leaf")
    placed = jnp.take(child.reshape(local_rows, all_cols, tile), inverse_order(col_map), axis=1)
    outbound = placed.reshape(1, local_rows, col_count * leaf_count, col_width)
    arrived = lax.all_to_all(outbound, ("col", "leaf"), split_axis=2, concat_axis=0, tiled=True)
    grouped = arrived.reshape(row_tiles, tile, col_width)
    relaid = jnp.take(grouped, inverse_order(row_map[0]), axis=0).reshape(
        row_tiles * tile, col_width
    )
    x_whole, w_whole = (
        lax.all_gather(x_fac, ("col", "leaf"), axis=1, tiled=True),
        lax.all_gather(w_fac, ("col", "leaf"), axis=1, tiled=True),
    )
    v_whole, z_whole = (
        lax.all_gather(v_fac, "row", axis=1, tiled=True),
        lax.all_gather(z_fac, "row", axis=1, tiled=True),
    )
    x_three = x_whole.reshape(row_tiles, RMAX, tile)
    w_three = w_whole.reshape(row_tiles, RMAX, tile)
    v_three = v_whole.reshape(col_tiles, RMAX, tile)
    z_three = z_whole.reshape(col_tiles, RMAX, tile)
    dv = jnp.einsum("kb,jrb->jkr", dinv, v_three, precision=highest)
    permuted = jnp.take(w_three, pivots, axis=2)
    core = jnp.einsum("irk,jks->ijrs", permuted, dv, precision=highest)
    rank_index = jnp.arange(RMAX, dtype=jnp.int32)
    dense_tile = (admissible == 0)[:, :, None]
    keep_rows = (rank_index[None, None, :] < rank_rows[:, None, None]) | dense_tile
    keep_cols = (rank_index[None, None, :] < rank_cols[None, :, None]) | dense_tile
    core = jnp.where(keep_rows[:, :, :, None] & keep_cols[:, :, None, :], core, jnp.float32(0.0))
    left = jnp.einsum("irb,ijrs->ibjs", x_three, core, precision=highest)
    update = jnp.einsum("ibjs,jsc->ibjc", left, z_three, precision=highest).reshape(
        row_tiles * tile, col_width
    )
    return front + relaid - update


def solution(mesh):
    return jax.shard_map(
        on_device,
        mesh=mesh,
        in_specs=(
            P("row", ("col", "leaf")),
            P(("row", "col", "leaf"), None),
            P("row", None),
            P(),
            P("row", ("col", "leaf")),
            P("row", ("col", "leaf")),
            P(("col", "leaf"), "row"),
            P(("col", "leaf"), "row"),
            P(),
            P(),
            P("row"),
            P(("col", "leaf")),
            P("row", ("col", "leaf")),
        ),
        out_specs=P("row", ("col", "leaf")),
        check_vma=False,
    )
```

profile of v0, /device:TPU:1, one launch (start us, length us, event | category | flops | bytes accessed | tf_op | source)
XLA Modules:
  0.0 322.9 jit_solution(7695282449139520069)
XLA Ops:
  0.0 0.7 compare_select_fusion.2
  0.7 0.8 scatter_custom_fusion.1
  1.5 4.8 %copy.71 = f32[8,64,8,256]{3,2,0,1:T(8,128)} copy(f32[8,64,8,256]{3,2,1,0:T(8,128)} %bitcast.71) | data formatting | bytes 8388608 | tf_op jit(solution)/shard_map/reshape | solution.py:38
  6.3 4.9 %gather_fusion = f32[64,64,256]{2,1,0:T(8,128)} fusion(f32[64,64,256]{2,0,1:T(8,128)} %bitcast.69, s32[1024]{0:T(1024)S(1)} %pad_clamp_fusion.2), kind=kCustom, calls=%fused_computation | custom fusion | bytes 8388864 | tf_op jit(solution)/shard_map/jit(_take)/gather | solution.py:38
  11.3 6.6 %copy.32 = f32[64,64,256]{2,1,0:T(8,128)} copy(f32[64,64,256]{2,0,1:T(8,128)} %bitcast.67) | data formatting | bytes 8388608 | tf_op jit(solution)/shard_map/jit(_take)/gather | solution.py:38
  17.9 5.2 %gather.17 = f32[1,64,32,512]{3,2,1,0:T(8,128)} reshape(f32[64,64,256]{2,1,0:T(8,128)} %copy.32) | data formatting | bytes 8388608 | tf_op jit(solution)/shard_map/jit(_take)/gather | solution.py:38
  23.4 2.8 broadcast_select_fusion
  26.2 4.4 %copy.33 = f32[1,64,32,512]{3,1,0,2:T(8,128)} copy(f32[1,64,32,512]{3,2,1,0:T(8,128)S(1)} %broadcast_select_fusion) | data formatting | bytes 8388608 | tf_op jit(solution)/shard_map/jit(_take)/select_n | solution.py:38
  30.6 12.8 %all-to-all-start = ((f32[1,64,32,512]{3,1,0,2:T(8,128)}), f32[1,64,32,512]{3,1,0,2:T(8,128)}, u32[]{:S(2)}, u32[]{:S(2)}) async-start(f32[1,64,32,512]{3,1,0,2:T(8,128)} %copy.33), calls=%async_computation | async-start | bytes 8388608 | tf_op jit(solution)/shard_map/all_to_all | solution.py:40
  43.5 129.5 %all_gather.13 = f32[8,16384]{1,0:T(8,128)S(1)} all-gather(f32[8,512]{1,0:T(8,128)S(1)} %copy-done.2), channel_id=1, replica_groups=mesh['row'=8,'col'=16,'leaf'=2] {'col','leaf'}, dimensions={1}, use_global_device_ids=true | all-gather | bytes 540672 | tf_op jit(solution)/shard_map/all_gather | solution.py:47
  173.6 1.0 gather_fusion.2
  174.7 22.0 %all_gather.12 = f32[2,16384]{1,0:T(2,128)S(1)} all-gather(f32[2,2048]{1,0:T(2,128)S(1)} %copy-done.3), channel_id=1, replica_groups=mesh['row'=8,'col'=16,'leaf'=2] {'row'}, dimensions={1}, use_global_device_ids=true | all-gather | bytes 147456 | tf_op jit(solution)/shard_map/all_gather | solution.py:50
  196.7 21.8 %all_gather.15 = f32[2,16384]{1,0:T(2,128)S(1)} all-gather(f32[2,2048]{1,0:T(2,128)S(1)} %copy-done.4), channel_id=1, replica_groups=mesh['row'=8,'col'=16,'leaf'=2] {'row'}, dimensions={1}, use_global_device_ids=true | all-gather | bytes 147456 | tf_op jit(solution)/shard_map/all_gather | solution.py:51
  219.1 54.4 %all_gather.14 = f32[8,16384]{1,0:T(8,128)S(1)} all-gather(f32[8,512]{1,0:T(8,128)S(1)} %copy-done.5), channel_id=1, replica_groups=mesh['row'=8,'col'=16,'leaf'=2] {'col','leaf'}, dimensions={1}, use_global_device_ids=true | all-gather | bytes 540672 | tf_op jit(solution)/shard_map/all_gather | solution.py:46
  273.9 0.9 fusion
  274.8 1.1 convolution_bitcast_fusion.1
  275.9 5.0 %convolution_bitcast_fusion = f32[8,256,2,256]{3,1,0,2:T(8,128)} fusion(f32[8,256,2,64]{1,3,0,2:T(8,128)S(1)} %convolution_bitcast_fusion.1, f32[1,2,64,256]{3,1,2,0:T(2,128)S(1)} %bitcast.76), kind=kOutput, calls=%fused_computation.7 | convolution fusion | flops 805306368 | bytes 5373952 | tf_op jit(solution)/shard_map/ibjs,jsc->ibjc/dot_general | solution.py:66
  280.9 5.5 %copy.40 = f32[8,256,2,256]{1,0,3,2:T(8,128)} copy(f32[8,256,2,256]{3,1,0,2:T(8,128)} %convolution_bitcast_fusion) | data formatting | bytes 8388608 | tf_op jit(solution)/shard_map/ibjs,jsc->ibjc/transpose | solution.py:66
  286.4 6.2 %copy.52 = f32[64,8,8,256]{3,1,2,0:T(8,128)} copy(f32[64,8,8,256]{3,2,1,0:T(8,128)} %bitcast.70) | data formatting | bytes 8388608
  293.3 5.4 %copy.35 = f32[2048,512]{0,1:T(8,128)} copy(f32[2048,512]{1,0:T(8,128)} %param.13) | data formatting | bytes 8388608 | tf_op args[0]
  298.7 5.0 %gather_fusion.1 = f32[8,256,512]{2,1,0:T(8,128)} fusion(f32[8,256,512]{2,1,0:T(8,128)} %bitcast.5, s32[1024]{0:T(1024)S(1)} %pad_clamp_fusion.1), kind=kCustom, calls=%fused_computation.1 | custom fusion | bytes 8388640 | tf_op jit(solution)/shard_map/jit(_take)/gather | solution.py:42
  303.7 5.4 %copy.34 = f32[2048,512]{0,1:T(8,128)} copy(f32[2048,512]{1,0:T(8,128)} %bitcast.68) | data formatting | bytes 8388608 | tf_op jit(solution)/shard_map/jit(_take)/gather | solution.py:42
  309.1 8.5 %add_subtract_fusion = f32[2048,512]{0,1:T(8,128)} fusion(f32[2048,512]{0,1:T(8,128)} %bitcast.66, f32[2048,512]{0,1:T(8,128)} %copy.35, f32[2048,512]{0,1:T(8,128)} %copy.34, pred[2048]{0:T(1024)(128)(4,1)S(1)} %broadcast_in_dim.62), kind=kLoop, calls=%fused_computation.6 | loop fusion | flops 3145728 | bytes 16779264 | tf_op jit(solution)/shard_map/sub | solution.py:69
  317.5 5.3 %copy.41 = f32[2048,512]{1,0:T(8,128)} copy(f32[2048,512]{0,1:T(8,128)} %add_subtract_fusion) | data formatting | bytes 8388608 | tf_op jit(solution)/shard_map/sub | solution.py:69
  (50 shorter events, 2.7 us)
Async XLA Ops:
  0.0 218.5 %copy-start = (f32[256,256]{1,0:T(8,128)S(1)}, f32[256,256]{1,0:T(8,128)}, u32[]{:S(2)}) copy-start(f32[256,256]{1,0:T(8,128)} %param.21) | copy-start | bytes 786436
  30.6 12.8 %copy-start.7 = (s32[8,2]{0,1:T(2,128)S(1)}, s32[8,2]{0,1:T(2,128)}, u32[]{:S(2)}) copy-start(s32[8,2]{0,1:T(2,128)} %param.25) | copy-start | bytes 196
  30.6 13.0 %copy-start.2 = (f32[8,512]{1,0:T(8,128)S(1)}, f32[8,512]{1,0:T(8,128)}, u32[]{:S(2)}) copy-start(f32[8,512]{1,0:T(8,128)} %param.18) | copy-start | bytes 49156
  30.6 143.0 %copy-start.6 = (s32[256]{0:T(256)S(1)}, s32[256]{0:T(256)}, u32[]{:S(2)}) copy-start(s32[256]{0:T(256)} %param.22) | copy-start | bytes 3076
  30.6 268.2 %all-to-all-start = ((f32[1,64,32,512]{3,1,0,2:T(8,128)}), f32[1,64,32,512]{3,1,0,2:T(8,128)}, u32[]{:S(2)}, u32[]{:S(2)}) async-start(f32[1,64,32,512]{3,1,0,2:T(8,128)} %copy.33), calls=%async_computation | async-start | bytes 8388608 | tf_op jit(solution)/shard_map/all_to_all | solution.py:40
  43.4 131.3 %copy-start.3 = (f32[2,2048]{1,0:T(2,128)S(1)}, f32[2,2048]{1,0:T(2,128)}, u32[]{:S(2)}) copy-start(f32[2,2048]{1,0:T(2,128)} %param.19) | copy-start | bytes 49156
  43.4 153.3 %copy-start.4 = (f32[2,2048]{1,0:T(2,128)S(1)}, f32[2,2048]{1,0:T(2,128)}, u32[]{:S(2)}) copy-start(f32[2,2048]{1,0:T(2,128)} %param.20) | copy-start | bytes 49156
  43.4 175.5 %copy-start.8 = (s32[2]{0:T(128)S(1)}, s32[2]{0:T(128)}, u32[]{:S(2)}) copy-start(s32[2]{0:T(128)} %param.24) | copy-start | bytes 28
  43.4 175.6 %copy-start.9 = (s32[8]{0:T(128)S(1)}, s32[8]{0:T(128)}, u32[]{:S(2)}) copy-start(s32[8]{0:T(128)} %param.23) | copy-start | bytes 100
  43.4 175.7 %copy-start.5 = (f32[8,512]{1,0:T(8,128)S(1)}, f32[8,512]{1,0:T(8,128)}, u32[]{:S(2)}) copy-start(f32[8,512]{1,0:T(8,128)} %param.17) | copy-start | bytes 49156
  286.4 6.2 %copy-start.10 = (s32[1,8]{1,0:T(1,128)S(1)}, s32[1,8]{1,0:T(1,128)}, u32[]{:S(2)}) copy-start(s32[1,8]{1,0:T(1,128)} %param.15) | copy-start | bytes 100
  309.1 13.8 %copy-start.1 = (f32[256,256]{1,0:T(8,128)S(1)}, f32[256,256]{1,0:T(8,128)}, u32[]{:S(2)}) copy-start(f32[256,256]{1,0:T(8,128)} %param.21) | copy-start | bytes 786436
where the time goes:
time: 324 us; the launch traced here: 323 us
  blocking collectives  228 us (70%)
  local copies, waits for them, and re-layouts  62.2 us (19%)
  starting transfers between devices  12.8 us (4%)
  other arithmetic  12.6 us (4%)
  matrix products  7.41 us (2%)
    all_gather x1, blocking collectives, on_device(): lax.all_gather(w_fac, ('col', 'leaf'), axis=1, tiled=True)  129 us
    all_gather x1, blocking collectives, on_device(): lax.all_gather(x_fac, ('col', 'leaf'), axis=1, tiled=True)  54.4 us
    all_gather x1, blocking collectives, on_device(): lax.all_gather(v_fac, 'row', axis=1, tiled=True)  22 us
    all_gather x1, blocking collectives, on_device(): lax.all_gather(z_fac, 'row', axis=1, tiled=True)  21.8 us
    gather x3, local copies, waits for them, and re-layouts, on_device(): jnp.take(child.reshape(local_rows, all_cols, tile), inverse_order(col_map...  16.8 us
    all_to_all x1, starting transfers between devices, on_device(): lax.all_to_all(outbound, ('col', 'leaf'), split_axis=2, concat_axis=0, ti...  12.8 us
    unnamed x26, local copies, waits for them, and re-layouts  11.8 us
    gather x2, local copies, waits for them, and re-layouts, on_device(): jnp.take(grouped, inverse_order(row_map[0]), axis=0)  10.3 us
  transfers between devices with their start and end apart: 1, of which 0 were waited for; matrix products, arithmetic and copies ran while one was open for 9% of the time, Pallas kernels for 0%

commit v1 on v0

--- a/solution.py
+++ b/solution.py
@@ -44,7 +44,15 @@
     )
     x_whole, w_whole = (
         lax.all_gather(x_fac, ("col", "leaf"), axis=1, tiled=True),
-        lax.all_gather(w_fac, ("col", "leaf"), axis=1, tiled=True),
+        jnp.concatenate(
+            jax.lax.all_to_all(
+                jnp.stack([w_fac for _ in range(jax.lax.axis_size(("col", "leaf")))]),
+                concat_axis=0,
+                axis_name=("col", "leaf"),
+                split_axis=0,
+            ),
+            1,
+        ),
     )
     v_whole, z_whole = (
         lax.all_gather(v_fac, "row", axis=1, tiled=True),

time: 324 us -> 292 us (0.901)
  blocking collectives: 228 us -> 185 us
  starting transfers between devices: 12.8 us -> 22.6 us
    all_gather x1 -> x0, blocking collectives: 129 us -> none  [on_device(): lax.all_gather(w_fac, ('col', 'leaf'), axis=1, tiled=True)]
    all_gather x1, blocking collectives: 22 us -> 103 us  [on_device(): lax.all_gather(v_fac, 'row', axis=1, tiled=True)]
    all_to_all x0 -> x1, starting transfers between devices: none -> 12.6 us  [on_device(): jax.lax.all_to_all(jnp.stack([w_fac for _ in range(jax.lax.axis_size(('co...]
    all_gather x1, blocking collectives: 54.4 us -> 59.9 us  [on_device(): lax.all_gather(x_fac, ('col', 'leaf'), axis=1, tiled=True)]
    unnamed x26 -> x23, local copies, waits for them, and re-layouts: 11.8 us -> 11.6 us
  transfers between devices with their start and end apart: 1 -> 2, of which waited for: 0 -> 0; matrix products, arithmetic and copies ran while one was open for 9% -> 20% of each run, Pallas kernels for 0% -> 0%
where the time goes in v1:
time: 292 us
  blocking collectives  185 us (63%)
  local copies, waits for them, and re-layouts  64 us (22%)
  starting transfers between devices  22.6 us (8%)
  other arithmetic  12.5 us (4%)
  matrix products  7.42 us (3%)
    all_gather x1, blocking collectives, on_device(): lax.all_gather(v_fac, 'row', axis=1, tiled=True)  103 us
    all_gather x1, blocking collectives, on_device(): lax.all_gather(x_fac, ('col', 'leaf'), axis=1, tiled=True)  59.9 us
    all_gather x1, blocking collectives, on_device(): lax.all_gather(z_fac, 'row', axis=1, tiled=True)  21.8 us
    gather x3, local copies, waits for them, and re-layouts, on_device(): jnp.take(child.reshape(local_rows, all_cols, tile), inverse_order(col_map...  16.8 us
    all_to_all x1, starting transfers between devices, on_device(): jax.lax.all_to_all(jnp.stack([w_fac for _ in range(jax.lax.axis_size(('co...  12.6 us
    unnamed x23, local copies, waits for them, and re-layouts  11.6 us
    gather x2, local copies, waits for them, and re-layouts, on_device(): jnp.take(grouped, inverse_order(row_map[0]), axis=0)  10.4 us
    all_to_all x1, starting transfers between devices, on_device(): lax.all_to_all(outbound, ('col', 'leaf'), split_axis=2, concat_axis=0, ti...  9.97 us
  transfers between devices with their start and end apart: 2, of which 0 were waited for; matrix products, arithmetic and copies ran while one was open for 20% of the time, Pallas kernels for 0%

profile of v1, /device:TPU:1, one launch (start us, length us, event | category | flops | bytes accessed | tf_op | source)
XLA Modules:
  0.0 291.6 jit_solution(5892506172598094769)
XLA Ops:
  0.0 1.6 stack.2
  1.6 12.6 %all-to-all-start.1 = ((f32[32,8,512]{2,1,0:T(8,128)}), f32[32,8,512]{2,1,0:T(8,128)S(1)}, u32[]{:S(2)}, u32[]{:S(2)}) async-start(f32[32,8,512]{2,1,0:T(8,128)} %stack.2), calls=%async_computation.1 | async-start | bytes 1048576 | tf_op jit(solution)/shard_map/all_to_all | solution.py:48
  14.9 4.8 %copy.71 = f32[8,64,8,256]{3,2,0,1:T(8,128)} copy(f32[8,64,8,256]{3,2,1,0:T(8,128)} %bitcast.68) | data formatting | bytes 8388608 | tf_op jit(solution)/shard_map/reshape | solution.py:38
  19.7 0.8 scatter_custom_fusion.1
  20.5 5.0 %gather_fusion = f32[64,64,256]{2,1,0:T(8,128)} fusion(f32[64,64,256]{2,0,1:T(8,128)} %bitcast.64, s32[1024]{0:T(1024)S(1)} %pad_clamp_fusion.2), kind=kCustom, calls=%fused_computation | custom fusion | bytes 8388864 | tf_op jit(solution)/shard_map/jit(_take)/gather | solution.py:38
  25.5 6.6 %copy.33 = f32[64,64,256]{2,1,0:T(8,128)} copy(f32[64,64,256]{2,0,1:T(8,128)} %bitcast.65) | data formatting | bytes 8388608 | tf_op jit(solution)/shard_map/jit(_take)/gather | solution.py:38
  32.1 5.2 %gather.17 = f32[1,64,32,512]{3,2,1,0:T(8,128)} reshape(f32[64,64,256]{2,1,0:T(8,128)} %copy.33) | data formatting | bytes 8388608 | tf_op jit(solution)/shard_map/jit(_take)/gather | solution.py:38
  37.6 2.8 broadcast_select_fusion
  40.3 4.4 %copy.34 = f32[1,64,32,512]{3,1,0,2:T(8,128)} copy(f32[1,64,32,512]{3,2,1,0:T(8,128)S(1)} %broadcast_select_fusion) | data formatting | bytes 8388608 | tf_op jit(solution)/shard_map/jit(_take)/select_n | solution.py:38
  44.7 10.0 %all-to-all-start = ((f32[1,64,32,512]{3,1,0,2:T(8,128)}), f32[1,64,32,512]{3,1,0,2:T(8,128)}, u32[]{:S(2)}, u32[]{:S(2)}) async-start(f32[1,64,32,512]{3,1,0,2:T(8,128)} %copy.34), calls=%async_computation | async-start | bytes 8388608 | tf_op jit(solution)/shard_map/all_to_all | solution.py:40
  55.6 5.4 %copy.36 = f32[2048,512]{0,1:T(8,128)} copy(f32[2048,512]{1,0:T(8,128)} %param.13) | data formatting | bytes 8388608 | tf_op args[0]
  61.1 103.1 %all_gather.9 = f32[2,16384]{1,0:T(2,128)S(1)} all-gather(f32[2,2048]{1,0:T(2,128)S(1)} %copy-done.2), channel_id=1, replica_groups=mesh['row'=8,'col'=16,'leaf'=2] {'row'}, dimensions={1}, use_global_device_ids=true | all-gather | bytes 147456 | tf_op jit(solution)/shard_map/all_gather | solution.py:58
  164.2 21.8 %all_gather.11 = f32[2,16384]{1,0:T(2,128)S(1)} all-gather(f32[2,2048]{1,0:T(2,128)S(1)} %copy-done.3), channel_id=1, replica_groups=mesh['row'=8,'col'=16,'leaf'=2] {'row'}, dimensions={1}, use_global_device_ids=true | all-gather | bytes 147456 | tf_op jit(solution)/shard_map/all_gather | solution.py:59
  186.7 59.9 %all_gather.10 = f32[8,16384]{1,0:T(8,128)S(1)} all-gather(f32[8,512]{1,0:T(8,128)S(1)} %copy-done.4), channel_id=1, replica_groups=mesh['row'=8,'col'=16,'leaf'=2] {'col','leaf'}, dimensions={1}, use_global_device_ids=true | all-gather | bytes 540672 | tf_op jit(solution)/shard_map/all_gather | solution.py:46
  247.4 1.0 gather_fusion.2
  248.8 0.9 fusion
  249.7 1.1 convolution_bitcast_fusion.1
  250.8 5.0 %convolution_bitcast_fusion = f32[8,256,2,256]{3,1,0,2:T(8,128)} fusion(f32[8,256,2,64]{1,3,0,2:T(8,128)S(1)} %convolution_bitcast_fusion.1, f32[1,2,64,256]{3,1,2,0:T(2,128)S(1)} %bitcast.72), kind=kOutput, calls=%fused_computation.7 | convolution fusion | flops 805306368 | bytes 5373952 | tf_op jit(solution)/shard_map/ibjs,jsc->ibjc/dot_general | solution.py:74
  255.8 5.4 %copy.42 = f32[8,256,2,256]{1,0,3,2:T(8,128)} copy(f32[8,256,2,256]{3,1,0,2:T(8,128)} %convolution_bitcast_fusion) | data formatting | bytes 8388608 | tf_op jit(solution)/shard_map/ibjs,jsc->ibjc/transpose | solution.py:74
  261.3 6.2 %copy.53 = f32[64,8,8,256]{3,1,2,0:T(8,128)} copy(f32[64,8,8,256]{3,2,1,0:T(8,128)} %bitcast.67) | data formatting | bytes 8388608
  267.4 5.0 %gather_fusion.1 = f32[8,256,512]{2,1,0:T(8,128)} fusion(f32[8,256,512]{2,1,0:T(8,128)} %bitcast.5, s32[1024]{0:T(1024)S(1)} %pad_clamp_fusion.1), kind=kCustom, calls=%fused_computation.1 | custom fusion | bytes 8388640 | tf_op jit(solution)/shard_map/jit(_take)/gather | solution.py:42
  272.4 5.4 %copy.35 = f32[2048,512]{0,1:T(8,128)} copy(f32[2048,512]{1,0:T(8,128)} %bitcast.66) | data formatting | bytes 8388608 | tf_op jit(solution)/shard_map/jit(_take)/gather | solution.py:42
  277.8 8.4 %add_subtract_fusion = f32[2048,512]{0,1:T(8,128)} fusion(f32[2048,512]{0,1:T(8,128)} %bitcast.63, f32[2048,512]{0,1:T(8,128)} %copy.36, f32[2048,512]{0,1:T(8,128)} %copy.35, pred[2048]{0:T(1024)(128)(4,1)S(1)} %broadcast_in_dim.62), kind=kLoop, calls=%fused_computation.6 | loop fusion | flops 3145728 | bytes 16779264 | tf_op jit(solution)/shard_map/sub | solution.py:77
  286.3 5.3 %copy.43 = f32[2048,512]{1,0:T(8,128)} copy(f32[2048,512]{0,1:T(8,128)} %add_subtract_fusion) | data formatting | bytes 8388608 | tf_op jit(solution)/shard_map/sub | solution.py:77
  (51 shorter events, 3.6 us)
Async XLA Ops:
  0.0 186.0 %copy-start = (f32[256,256]{1,0:T(8,128)S(1)}, f32[256,256]{1,0:T(8,128)}, u32[]{:S(2)}) copy-start(f32[256,256]{1,0:T(8,128)} %param.21) | copy-start | bytes 786436
  1.6 43.1 %all-to-all-start.1 = ((f32[32,8,512]{2,1,0:T(8,128)}), f32[32,8,512]{2,1,0:T(8,128)S(1)}, u32[]{:S(2)}, u32[]{:S(2)}) async-start(f32[32,8,512]{2,1,0:T(8,128)} %stack.2), calls=%async_computation.1 | async-start | bytes 1048576 | tf_op jit(solution)/shard_map/all_to_all | solution.py:48
  44.7 10.0 %copy-start.6 = (s32[8,2]{0,1:T(2,128)S(1)}, s32[8,2]{0,1:T(2,128)}, u32[]{:S(2)}) copy-start(s32[8,2]{0,1:T(2,128)} %param.25) | copy-start | bytes 196
  44.7 10.1 %copy-start.7 = (s32[1,8]{1,0:T(1,128)S(1)}, s32[1,8]{1,0:T(1,128)}, u32[]{:S(2)}) copy-start(s32[1,8]{1,0:T(1,128)} %param.15) | copy-start | bytes 100
  44.7 222.7 %all-to-all-start = ((f32[1,64,32,512]{3,1,0,2:T(8,128)}), f32[1,64,32,512]{3,1,0,2:T(8,128)}, u32[]{:S(2)}, u32[]{:S(2)}) async-start(f32[1,64,32,512]{3,1,0,2:T(8,128)} %copy.34), calls=%async_computation | async-start | bytes 8388608 | tf_op jit(solution)/shard_map/all_to_all | solution.py:40
  55.6 5.5 %copy-start.2 = (f32[2,2048]{1,0:T(2,128)S(1)}, f32[2,2048]{1,0:T(2,128)}, u32[]{:S(2)}) copy-start(f32[2,2048]{1,0:T(2,128)} %param.19) | copy-start | bytes 49156
  55.6 108.6 %copy-start.3 = (f32[2,2048]{1,0:T(2,128)S(1)}, f32[2,2048]{1,0:T(2,128)}, u32[]{:S(2)}) copy-start(f32[2,2048]{1,0:T(2,128)} %param.20) | copy-start | bytes 49156
  55.6 130.4 %copy-start.5 = (s32[256]{0:T(256)S(1)}, s32[256]{0:T(256)}, u32[]{:S(2)}) copy-start(s32[256]{0:T(256)} %param.22) | copy-start | bytes 3076
  55.6 130.8 %copy-start.8 = (s32[2]{0:T(128)S(1)}, s32[2]{0:T(128)}, u32[]{:S(2)}) copy-start(s32[2]{0:T(128)} %param.24) | copy-start | bytes 28
  55.6 130.9 %copy-start.9 = (s32[8]{0:T(128)S(1)}, s32[8]{0:T(128)}, u32[]{:S(2)}) copy-start(s32[8]{0:T(128)} %param.23) | copy-start | bytes 100
  55.6 131.1 %copy-start.4 = (f32[8,512]{1,0:T(8,128)S(1)}, f32[8,512]{1,0:T(8,128)}, u32[]{:S(2)}) copy-start(f32[8,512]{1,0:T(8,128)} %param.17) | copy-start | bytes 49156
  277.8 13.8 %copy-start.1 = (f32[256,256]{1,0:T(8,128)S(1)}, f32[256,256]{1,0:T(8,128)}, u32[]{:S(2)}) copy-start(f32[256,256]{1,0:T(8,128)} %param.21) | copy-start | bytes 786436
